TPU v7x, 128 devices: a whole 4x4x4 slice. The times are simulated.
128 devices in a mesh: grid: 8 (over x, core), proc: 16 (over z, y).
Axes of the slice: x: 4, y: 4, z: 4, core: 2. Of those that a mesh axis runs over, the one named last changes fastest.
Arguments:
- rhs: float32 [3, 8, 16, 256, 1024], P(None, 'grid', 'proc'), may hold values from -6 to 6
- tile_pairs: int32 [2, 8, 16, 32], P(None, 'grid', 'proc'), may hold values from -1 to 31, as said below
- tiles: bfloat16 [2, 8, 16, 32, 256, 256], P(None, 'grid', 'proc'), may hold values from -0.09375 to 0.09375
- dinv: float32 [3, 8, 16, 256, 256], P(None, 'grid', 'proc'), as said below
Outputs:
- solution: float32 [3, 8, 16, 256, 1024], P(None, 'grid', 'proc')
Inputs may be any that keep to these rules, and one draw needn't show every extreme that they name: tile_pairs[t, g, p] holds distinct pair numbers in its first slots and -1 in the others; pair number q names block column q mod 16 and destination q // 16 (0: the same grid, 1: the partner grid). In every transition and grid one device uses all 32 slots and the others use 2 to 16 of them. Each dinv tile is lower triangular with diagonal entries between 0.5 and 1.4.
All inputs are finite; a program needn't handle non-finite values.
Results may differ from a plain program's by a relative error of at most 0.0021.
Values may be sent and summed in bfloat16 or wider, within the bound.
No kernel may reach another device: no remote copies, remote signals or barrier semaphores. Data moves between devices by JAX's collectives and lax.ppermute only.
A program may use at most 128 MiB of HBM per device.

v0:
```python
import jax
import jax.numpy as jnp
from jax import lax
from jax.sharding import PartitionSpec as P


def from_partner(block, axis, apart):
    count = lax.axis_size(axis)
    route = []
    for low in range(count):
        high = low | 1 << apart
        if high != low and high < count:
            route += [(low, high), (high, low)]
    return lax.ppermute(block, axis, route)


def build_table(pairs, tile_set):
    slot_count = tile_set.shape[0]
    labels = lax.broadcasted_iota(jnp.int32, (slot_count, slot_count), 1)
    onehot = (pairs[:, None] == labels).astype(jnp.bfloat16)
    dense = jnp.einsum("sq,sij->qij", onehot, tile_set, preferred_element_type=jnp.float32)
    return dense.astype(jnp.bfloat16).reshape(
        2, slot_count // 2, tile_set.shape[1], tile_set.shape[2]
    )


def diagonal_solve(factor, values):
    return jnp.dot(
        factor, values, precision=lax.Precision.HIGHEST, preferred_element_type=jnp.float32
    )


def solve_levels(rhs_block, dinv_block, tables):
    levels = rhs_block.shape[0]
    current = diagonal_solve(dinv_block[0], rhs_block[0])
    solved = [current]
    for height in range(1, levels):
        dense_table = tables[height - 1]
        outgoing = current.astype(jnp.bfloat16)[None]
        partial_value = jnp.einsum(
            "dkij,kjr->dir",
            dense_table,
            lax.all_gather(outgoing, "proc", axis=0, tiled=True),
            preferred_element_type=jnp.float32,
        )
        partner = from_partner(partial_value[1], "grid", height - 1)
        update = partial_value[0] + partner
        current = diagonal_solve(dinv_block[height], rhs_block[height] - update)
        solved.append(current)
    return jnp.stack(solved)


def body(rhs, tile_pairs, tiles, dinv):
    rhs_block = rhs[:, 0, 0]
    dinv_block = dinv[:, 0, 0]
    tables = [
        build_table(tile_pairs[number, 0, 0], tiles[number, 0, 0])
        for number in range(tile_pairs.shape[0])
    ]
    solved = solve_levels(rhs_block, dinv_block, tables)
    return solved[:, None, None]


def solution(mesh):
    return jax.shard_map(
        body,
        mesh=mesh,
        in_specs=(
            P(None, "grid", "proc", None, None),
            P(None, "grid", "proc", None),
            P(None, "grid", "proc", None, None, None),
            P(None, "grid", "proc", None, None),
        ),
        out_specs=P(None, "grid", "proc", None, None),
        check_vma=False,
    )
```

profile of v0, /device:TPU:0, one launch (start us, length us, event | category | flops | bytes accessed | tf_op | source)
XLA Modules:
  0.0 222.2 jit_solution(5536468738525607536)
XLA Ops:
  6.5 0.0 all-gather.5.cloned.1.call-start
  6.5 3.1 %fusion.41 = (bf16[256,1024]{1,0:T(8,128)(2,1)}, f32[256,1024]{1,0:T(8,128)S(1)}) fusion(f32[3,1,1,256,1024]{4,3,2,1,0:T(8,128)} %param.4, f32[3,1,1,256,256]{4,3,2,1,0:T(8,128)} %param.7), kind=kOutput, calls=%fused_computation.46 | convolution fusion | flops 805568512 | bytes 2883584 | tf_op jit(solution)/shard_map/dot_general | solution.py:28
  9.7 0.0 all-gather.5.cloned.1.call-update
  9.7 0.0 all-gather.7.cloned.1.call-start
  9.7 0.7 slice_bitcast_fusion.4
  10.4 5.2 %fusion.40 = (bf16[1,1,1,32,256,256]{5,4,3,2,1,0:T(8,128)(2,1)}, bf16[1,1,1,32,256,256]{5,4,3,2,1,0:T(8,128)(2,1)S(1)}) fusion(bf16[2,1,1,32,256,256]{5,4,3,2,1,0:T(8,128)(2,1)} %param.6), kind=kLoop, calls=%fused_computation.45 | loop fusion | bytes 16777216 | tf_op jit(solution)/shard_map/slice | solution.py:57
  15.6 4.6 %fusion.6 = bf16[32,256,256]{2,0,1:T(8,128)(2,1)} fusion(bf16[1,1,1,32,256,256]{5,4,3,2,1,0:T(8,128)(2,1)S(1)} %get-tuple-element.6, s32[32]{0:T(128)S(1)} %get-tuple-element.8), kind=kOutput, calls=%fused_computation.9 | convolution fusion | flops 136315904 | bytes 8388736 | tf_op jit(solution)/shard_map/sq,sij->qij/dot_general | solution.py:21
  20.2 63.1 %all-gather.5.cloned.1.call-done = bf16[4096,1024]{1,0:T(8,128)(2,1)} async-done(((bf16[256,1024]{1,0:T(8,128)(2,1)}), bf16[4096,1024]{1,0:T(8,128)(2,1)}) %all-gather.5.cloned.1.call-update) | async-done | bytes 8388624 | tf_op jit(solution)/shard_map/all_gather | solution.py:43
  83.3 0.0 copy-start
  83.3 13.0 %fusion.8 = f32[2,256,1024]{2,1,0:T(8,128)S(1)} fusion(bf16[16,256,1024,1]{2,1,0,3:T(8,128)(2,1)} %bitcast.103, bf16[2,16,256,256]{3,1,0,2:T(8,128)(2,1)} %bitcast.99), kind=kOutput, calls=%fused_computation.11 | convolution fusion | flops 4294967296 | bytes 14680064 | tf_op jit(solution)/shard_map/dkij,kjr->dir/dot_general | solution.py:40
  96.3 0.1 slice_bitcast_fusion.2
  96.4 0.3 collective-permute-start
  96.6 2.6 %collective-permute-done = f32[256,1024]{1,0:T(8,128)S(1)} collective-permute-done((f32[256,1024]{1,0:T(8,128)S(1)}, f32[256,1024]{1,0:T(8,128)S(1)}, u32[]{:S(2)}, u32[]{:S(2)}) %collective-permute-start) | collective-permute-done | bytes 1048608 | tf_op jit(solution)/shard_map/ppermute | solution.py:14
  99.3 0.0 copy-done
  99.3 3.2 %bitcast_convert_fusion = (bf16[256,1024]{1,0:T(8,128)(2,1)}, f32[1024,256]{0,1:T(8,128)S(1)}) fusion(f32[3,1,1,256,256]{4,3,2,1,0:T(8,128)S(1)} %copy-done, f32[256,1024]{1,0:T(8,128)S(1)} %collective-permute-done, f32[2,256,1024]{2,1,0:T(8,128)S(1)} %fusion.8, f32[3,1,1,256,1024]{4,3,2,1,0:T(8,128)} %param.4), kind=kOutput, calls=%fused_computation.24 | convolution fusion | flops 806092800 | bytes 4980736 | tf_op jit(solution)/shard_map/dot_general | solution.py:28
  102.5 0.0 all-gather.7.cloned.1.call-update
  102.5 6.8 %fusion.7 = bf16[32,256,256]{2,0,1:T(8,128)(2,1)} fusion(bf16[1,1,1,32,256,256]{5,4,3,2,1,0:T(8,128)(2,1)} %get-tuple-element.5, s32[32]{0:T(128)S(1)} %get-tuple-element.7), kind=kOutput, calls=%fused_computation.10 | convolution fusion | flops 136315904 | bytes 8388736 | tf_op jit(solution)/shard_map/sq,sij->qij/dot_general | solution.py:21
  109.3 63.9 %all-gather.7.cloned.1.call-done = bf16[4096,1024]{1,0:T(8,128)(2,1)} async-done(((bf16[256,1024]{1,0:T(8,128)(2,1)}), bf16[4096,1024]{1,0:T(8,128)(2,1)}) %all-gather.7.cloned.1.call-update) | async-done | bytes 8388624 | tf_op jit(solution)/shard_map/all_gather | solution.py:43
  173.2 12.9 %fusion.11 = f32[2,256,1024]{2,1,0:T(8,128)S(1)} fusion(bf16[16,256,1024,1]{2,1,0,3:T(8,128)(2,1)} %bitcast.104, bf16[2,16,256,256]{3,1,0,2:T(8,128)(2,1)} %bitcast.100), kind=kOutput, calls=%fused_computation.12 | convolution fusion | flops 4294967296 | bytes 14680064 | tf_op jit(solution)/shard_map/dkij,kjr->dir/dot_general | solution.py:40
  186.1 0.1 slice_bitcast_fusion
  186.2 1.5 collective-permute-start.1
  187.8 23.3 %collective-permute-done.1 = f32[256,1024]{1,0:T(8,128)S(1)} collective-permute-done((f32[256,1024]{1,0:T(8,128)S(1)}, f32[256,1024]{1,0:T(8,128)S(1)}, u32[]{:S(2)}, u32[]{:S(2)}) %collective-permute-start.1) | collective-permute-done | bytes 1048608 | tf_op jit(solution)/shard_map/ppermute | solution.py:14
  211.0 2.4 %convolution_bitcast_fusion = f32[1,256,1024]{2,1,0:T(8,128)S(1)} fusion(f32[256,1024]{1,0:T(8,128)S(1)} %collective-permute-done.1, f32[2,256,1024]{2,1,0:T(8,128)S(1)} %fusion.11, f32[3,1,1,256,1024]{4,3,2,1,0:T(8,128)} %param.4, f32[3,1,1,256,256]{4,3,2,1,0:T(8,128)S(1)} %copy-done), kind=kOutput, calls=%fused_computation.13 | convolution fusion | flops 805830656 | bytes 4456448 | tf_op jit(solution)/shard_map/dot_general | solution.py:28
  213.5 1.9 maximum_bitcast_fusion
Async XLA Ops:
  6.5 76.7 %all-gather.5.cloned.1.call-start = ((), (), s32[]{:S(2)}) async-start(), calls=%async_computation | async-start | bytes 8912896 | tf_op jit(solution)/shard_map/all_gather | solution.py:43
  9.7 163.5 %all-gather.7.cloned.1.call-start = ((), (), s32[]{:S(2)}) async-start(), calls=%async_computation.1 | async-start | bytes 8912896 | tf_op jit(solution)/shard_map/all_gather | solution.py:43
  83.3 16.0 %copy-start = (f32[3,1,1,256,256]{4,3,2,1,0:T(8,128)S(1)}, f32[3,1,1,256,256]{4,3,2,1,0:T(8,128)}, u32[]{:S(2)}) copy-start(f32[3,1,1,256,256]{4,3,2,1,0:T(8,128)} %param.7) | copy-start | bytes 2359300
  96.4 2.9 %collective-permute-start = (f32[256,1024]{1,0:T(8,128)S(1)}, f32[256,1024]{1,0:T(8,128)S(1)}, u32[]{:S(2)}, u32[]{:S(2)}) collective-permute-start(f32[256,1024]{1,0:T(8,128)S(1)} %slice_bitcast_fusion.2), channel_id=1, source_target_pairs={{0,16},{16,0},{32,48},{48,32},{64,80},{80,64},{96,112},{112,96},{1... | collective-permute-start | bytes 3145736 | tf_op jit(solution)/shard_map/ppermute | solution.py:14
  186.2 24.8 %collective-permute-start.1 = (f32[256,1024]{1,0:T(8,128)S(1)}, f32[256,1024]{1,0:T(8,128)S(1)}, u32[]{:S(2)}, u32[]{:S(2)}) collective-permute-start(f32[256,1024]{1,0:T(8,128)S(1)} %slice_bitcast_fusion), channel_id=1, source_target_pairs={{0,32},{32,0},{16,48},{48,16},{64,96},{96,64},{80,112},{112,80},{1... | collective-permute-start | bytes 3145736 | tf_op jit(solution)/shard_map/ppermute | solution.py:14
Sparse Core Ops, SparseCore 0:
  9.8 73.4 all-gather.4
  102.6 70.5 all-gather.6
where the time goes:
time: 222 us
  waiting for transfers between devices  153 us (69%)
  matrix products  45.9 us (21%)
  between operations  13.5 us (6%)
  local copies, waits for them, and re-layouts  6.09 us (3%)
    all_gather x2, waiting for transfers between devices, solve_levels(): lax.all_gather(outgoing, 'proc', axis=0, tiled=True)  127 us
    ppermute x2, waiting for transfers between devices, from_partner(): return lax.ppermute(block, axis, route)  25.9 us
    dot_general x2, matrix products, solve_levels(): jnp.einsum('dkij,kjr->dir', dense_table, lax.all_gather(outgoing, 'proc',...  25.9 us
    dot_general x2, matrix products, build_table(): jnp.einsum('sq,sij->qij', onehot, tile_set, preferred_element_type=jnp.fl...  11.3 us
    dot_general x3, matrix products, diagonal_solve(): jnp.dot(factor, values, precision=lax.Precision.HIGHEST, preferred_elemen...  8.76 us
    slice x1, local copies, waits for them, and re-layouts, body(): tiles[number, 0, 0]  5.2 us
  transfers between devices with their start and end apart: 4, of which 4 were waited for; matrix products, arithmetic and copies ran while one was open for 8% of the time, Pallas kernels for 0%

commit v1 on v0

--- a/solution.py
+++ b/solution.py
@@ -2,6 +2,13 @@
 import jax.numpy as jnp
 from jax import lax
 from jax.sharding import PartitionSpec as P
+
+
+def swapped_in(shard, name, along):
+    size = lax.axis_size(name)
+    blocks = jnp.stack([shard for _ in range(size)])
+    blocks = lax.all_to_all(blocks, name, split_axis=0, concat_axis=0)
+    return jnp.concatenate(blocks, axis=along)
 
 
 def from_partner(block, axis, apart):
@@ -40,7 +47,7 @@
         partial_value = jnp.einsum(
             "dkij,kjr->dir",
             dense_table,
-            lax.all_gather(outgoing, "proc", axis=0, tiled=True),
+            swapped_in(outgoing, "proc", 0),
             preferred_element_type=jnp.float32,
         )
         partner = from_partner(partial_value[1], "grid", height - 1)

time: 222 us -> 335 us (1.51)
  waiting for transfers between devices: 153 us -> 258 us
  starting transfers between devices: 1.86 us -> 15.8 us
  between operations: 13.5 us -> 0.1 us
  local copies, waits for them, and re-layouts: 6.09 us -> 14.1 us
    all_to_all x0 -> x2, waiting for transfers between devices: none -> 233 us  [swapped_in(): blocks = lax.all_to_all(blocks, name, split_axis=0, concat_axis=0)]
    all_gather x2 -> x0, waiting for transfers between devices: 127 us -> none  [solve_levels(): lax.all_gather(outgoing, 'proc', axis=0, tiled=True)]
    all_to_all x0 -> x2, starting transfers between devices: none -> 14 us  [swapped_in(): blocks = lax.all_to_all(blocks, name, split_axis=0, concat_axis=0)]
    another operation x0 -> x2, local copies, waits for them, and re-layouts: none -> 8.68 us  [swapped_in(): blocks = jnp.stack([shard for _ in range(size)])]
  transfers between devices with their start and end apart: 4 -> 4, of which waited for: 4 -> 4; matrix products, arithmetic and copies ran while one was open for 8% -> 5% of each run, Pallas kernels for 0% -> 0%
where the time goes in v1:
time: 335 us; the launch traced here: 334 us
  waiting for transfers between devices  258 us (77%)
  matrix products  44.5 us (13%)
  starting transfers between devices  15.8 us (5%)
  local copies, waits for them, and re-layouts  14.1 us (4%)
    all_to_all x2, waiting for transfers between devices, swapped_in(): blocks = lax.all_to_all(blocks, name, split_axis=0, concat_axis=0)  233 us
    dot_general x2, matrix products, solve_levels(): jnp.einsum('dkij,kjr->dir', dense_table, swapped_in(outgoing, 'proc', 0),...  25.9 us
    ppermute x2, waiting for transfers between devices, from_partner(): return lax.ppermute(block, axis, route)  25.3 us
    all_to_all x2, starting transfers between devices, swapped_in(): blocks = lax.all_to_all(blocks, name, split_axis=0, concat_axis=0)  14 us
    dot_general x2, matrix products, build_table(): jnp.einsum('sq,sij->qij', onehot, tile_set, preferred_element_type=jnp.fl...  11.4 us
    another operation x2, local copies, waits for them, and re-layouts, swapped_in(): blocks = jnp.stack([shard for _ in range(size)])  8.68 us
    dot_general x3, matrix products, diagonal_solve(): jnp.dot(factor, values, precision=lax.Precision.HIGHEST, preferred_elemen...  7.18 us
  transfers between devices with their start and end apart: 4, of which 4 were waited for; matrix products, arithmetic and copies ran while one was open for 5% of the time, Pallas kernels for 0%

profile of v1, /device:TPU:0, one launch (start us, length us, event | category | flops | bytes accessed | tf_op | source)
XLA Modules:
  0.0 334.4 jit_solution(13057985138132216624)
XLA Ops:
  0.0 2.3 fusion.47
  2.3 4.3 %stack.19 = bf16[16,1,256,1024]{3,2,1,0:T(8,128)(2,1)} broadcast(bf16[256,1024]{1,0:T(8,128)(2,1)S(1)} %get-tuple-element.9), dimensions={2,3} | broadcast | bytes 8912896 | tf_op jit(solution)/shard_map/stack | solution.py:9
  6.7 0.0 copy-start.1
  6.7 8.3 %all-to-all-start = ((bf16[16,1,256,1024]{3,2,1,0:T(8,128)(2,1)}), bf16[16,1,256,1024]{3,2,1,0:T(8,128)(2,1)}, u32[]{:S(2)}, u32[]{:S(2)}) async-start(bf16[16,1,256,1024]{3,2,1,0:T(8,128)(2,1)} %stack.19), calls=%async_computation | async-start | bytes 16777216 | tf_op jit(solution)/shard_map/all_to_all | solution.py:10
  15.0 0.0 copy-done.1
  15.1 5.2 %fusion.46 = (bf16[1,1,1,32,256,256]{5,4,3,2,1,0:T(8,128)(2,1)}, bf16[1,1,1,32,256,256]{5,4,3,2,1,0:T(8,128)(2,1)S(1)}) fusion(bf16[2,1,1,32,256,256]{5,4,3,2,1,0:T(8,128)(2,1)} %param.6), kind=kLoop, calls=%fused_computation.47 | loop fusion | bytes 16777216 | tf_op jit(solution)/shard_map/slice | solution.py:64
  20.3 4.6 %fusion.8 = bf16[32,256,256]{2,0,1:T(8,128)(2,1)} fusion(bf16[1,1,1,32,256,256]{5,4,3,2,1,0:T(8,128)(2,1)S(1)} %get-tuple-element.6, s32[32]{0:T(128)S(1)} %get-tuple-element.8), kind=kOutput, calls=%fused_computation.11 | convolution fusion | flops 136315904 | bytes 8388736 | tf_op jit(solution)/shard_map/sq,sij->qij/dot_general | solution.py:28
  24.9 114.3 %all-to-all-done = bf16[16,1,256,1024]{3,2,1,0:T(8,128)(2,1)} async-done(((bf16[16,1,256,1024]{3,2,1,0:T(8,128)(2,1)}), bf16[16,1,256,1024]{3,2,1,0:T(8,128)(2,1)}, u32[]{:S(2)}, u32[]{:S(2)}) %all-to-all-start) | async-done | bytes 8388640 | tf_op jit(solution)/shard_map/all_to_all | solution.py:10
  139.2 0.0 copy-start
  139.2 13.0 %fusion.10 = f32[2,256,1024]{2,1,0:T(8,128)S(1)} fusion(bf16[16,1,256,1024]{3,2,1,0:T(8,128)(2,1)} %all-to-all-done, bf16[2,16,256,256]{3,1,0,2:T(8,128)(2,1)} %bitcast.103), kind=kOutput, calls=%fused_computation.13 | convolution fusion | flops 4294967296 | bytes 14680064 | tf_op jit(solution)/shard_map/dkij,kjr->dir/dot_general | solution.py:47
  152.2 0.1 slice_bitcast_fusion.2
  152.3 0.3 collective-permute-start
  152.5 2.6 collective-permute-done
  155.2 0.0 copy-done
  155.2 2.4 bitcast_convert_fusion
  157.6 4.3 %stack.21 = bf16[16,1,256,1024]{3,2,1,0:T(8,128)(2,1)} broadcast(bf16[256,1024]{1,0:T(8,128)(2,1)S(1)} %get-tuple-element.11), dimensions={2,3} | broadcast | bytes 8912896 | tf_op jit(solution)/shard_map/stack | solution.py:9
  162.0 5.7 %all-to-all-start.1 = ((bf16[16,1,256,1024]{3,2,1,0:T(8,128)(2,1)}), bf16[16,1,256,1024]{3,2,1,0:T(8,128)(2,1)}, u32[]{:S(2)}, u32[]{:S(2)}) async-start(bf16[16,1,256,1024]{3,2,1,0:T(8,128)(2,1)} %stack.21), calls=%async_computation.1 | async-start | bytes 16777216 | tf_op jit(solution)/shard_map/all_to_all | solution.py:10
  167.6 6.8 %fusion.9 = bf16[32,256,256]{2,0,1:T(8,128)(2,1)} fusion(bf16[1,1,1,32,256,256]{5,4,3,2,1,0:T(8,128)(2,1)} %get-tuple-element.5, s32[32]{0:T(128)S(1)} %get-tuple-element.7), kind=kOutput, calls=%fused_computation.12 | convolution fusion | flops 136315904 | bytes 8388736 | tf_op jit(solution)/shard_map/sq,sij->qij/dot_general | solution.py:28
  174.4 118.5 %all-to-all-done.1 = bf16[16,1,256,1024]{3,2,1,0:T(8,128)(2,1)} async-done(((bf16[16,1,256,1024]{3,2,1,0:T(8,128)(2,1)}), bf16[16,1,256,1024]{3,2,1,0:T(8,128)(2,1)}, u32[]{:S(2)}, u32[]{:S(2)}) %all-to-all-start.1) | async-done | bytes 8388640 | tf_op jit(solution)/shard_map/all_to_all | solution.py:10
  292.9 12.9 %fusion.15 = f32[2,256,1024]{2,1,0:T(8,128)S(1)} fusion(bf16[16,1,256,1024]{3,2,1,0:T(8,128)(2,1)} %all-to-all-done.1, bf16[2,16,256,256]{3,1,0,2:T(8,128)(2,1)} %bitcast.104), kind=kOutput, calls=%fused_computation.14 | convolution fusion | flops 4294967296 | bytes 14680064 | tf_op jit(solution)/shard_map/dkij,kjr->dir/dot_general | solution.py:47
  305.8 0.1 slice_bitcast_fusion
  305.9 1.6 collective-permute-start.1
  307.5 22.6 %collective-permute-done.1 = f32[256,1024]{1,0:T(8,128)S(1)} collective-permute-done((f32[256,1024]{1,0:T(8,128)S(1)}, f32[256,1024]{1,0:T(8,128)S(1)}, u32[]{:S(2)}, u32[]{:S(2)}) %collective-permute-start.1) | collective-permute-done | bytes 1048608 | tf_op jit(solution)/shard_map/ppermute | solution.py:21
  330.1 2.4 convolution_bitcast_fusion
  332.6 1.9 maximum_bitcast_fusion
  (1 shorter events, 0.0 us)
Async XLA Ops:
  6.7 8.4 %copy-start.1 = (s32[2,1,1,32]{3,2,1,0:T(1,128)S(1)}, s32[2,1,1,32]{3,2,1,0:T(1,128)}, u32[]{:S(2)}) copy-start(s32[2,1,1,32]{3,2,1,0:T(1,128)} %param.5) | copy-start | bytes 772
  6.7 132.5 %all-to-all-start = ((bf16[16,1,256,1024]{3,2,1,0:T(8,128)(2,1)}), bf16[16,1,256,1024]{3,2,1,0:T(8,128)(2,1)}, u32[]{:S(2)}, u32[]{:S(2)}) async-start(bf16[16,1,256,1024]{3,2,1,0:T(8,128)(2,1)} %stack.19), calls=%async_computation | async-start | bytes 16777216 | tf_op jit(solution)/shard_map/all_to_all | solution.py:10
  139.2 16.0 %copy-start = (f32[3,1,1,256,256]{4,3,2,1,0:T(8,128)S(1)}, f32[3,1,1,256,256]{4,3,2,1,0:T(8,128)}, u32[]{:S(2)}) copy-start(f32[3,1,1,256,256]{4,3,2,1,0:T(8,128)} %param.7) | copy-start | bytes 2359300
  152.3 2.9 collective-permute-start
  162.0 131.0 %all-to-all-start.1 = ((bf16[16,1,256,1024]{3,2,1,0:T(8,128)(2,1)}), bf16[16,1,256,1024]{3,2,1,0:T(8,128)(2,1)}, u32[]{:S(2)}, u32[]{:S(2)}) async-start(bf16[16,1,256,1024]{3,2,1,0:T(8,128)(2,1)} %stack.21), calls=%async_computation.1 | async-start | bytes 16777216 | tf_op jit(solution)/shard_map/all_to_all | solution.py:10
  305.9 24.2 %collective-permute-start.1 = (f32[256,1024]{1,0:T(8,128)S(1)}, f32[256,1024]{1,0:T(8,128)S(1)}, u32[]{:S(2)}, u32[]{:S(2)}) collective-permute-start(f32[256,1024]{1,0:T(8,128)S(1)} %slice_bitcast_fusion), channel_id=1, source_target_pairs={{0,32},{32,0},{16,48},{48,16},{64,96},{96,64},{80,112},{112,80},{1... | collective-permute-start | bytes 3145736 | tf_op jit(solution)/shard_map/ppermute | solution.py:21
